TPU v7x, 32 devices: a whole 2x2x4 slice. The times are simulated.
32 devices in a mesh: grp: 1, row: 8 (over z, y), col: 2 (over x), ch: 2 (over core).
Axes of the slice: x: 2, y: 2, z: 4, core: 2. Of those that a mesh axis runs over, the one named last changes fastest.
Arguments:
- pair_input: float32 [96, 96, 128], P(('grp', 'row'), ('col', 'ch')), may hold values from -6 to 6
- saved_product: float32 [96, 96, 128], P(('grp', 'row'), ('col', 'ch')), may hold values from -6 to 6
- pair_grad: float32 [96, 96, 128], P(('grp', 'row'), ('col', 'ch')), may hold values from -6 to 6
- token_mask: int32 [96], P('grp'), may hold values 0 or 1
- w_one: float32 [128, 512], replicated, may hold values from -0.5 to 0.5
- w_two: float32 [128, 512], replicated, may hold values from -0.5 to 0.5
- w_three: float32 [512, 128], replicated, may hold values from -0.25 to 0.25
- w_left: float32 [128, 128], replicated, may hold values from -0.5 to 0.5
- w_left_gate: float32 [128, 128], replicated, may hold values from -0.5 to 0.5
- w_right: float32 [128, 128], replicated, may hold values from -0.5 to 0.5
- w_right_gate: float32 [128, 128], replicated, may hold values from -0.5 to 0.5
- w_out: float32 [128, 128], replicated, may hold values from -0.5 to 0.5
- w_out_gate: float32 [128, 128], replicated, may hold values from -0.5 to 0.5
Outputs:
- input_grad: float32 [96, 96, 128], P(('grp', 'row'), ('col', 'ch'))
All inputs are finite; a program needn't handle non-finite values.
Results may differ from a plain program's by a relative error of at most 0.0038.
Values may be sent and summed in bfloat16 or wider, within the bound.
A program may use at most 128 MiB of HBM per device.

v0:
```python
import jax
import jax.numpy as jnp
from jax import lax
from jax.sharding import PartitionSpec as P

epsilon = 1e-05


def from_root(value, axis, source):
    kept = jnp.where(lax.axis_index(axis) == source, value, 0).astype(value.dtype)
    return lax.psum(kept, axis)


def matmul(left, right):
    return jnp.dot(left, right, precision=lax.Precision.HIGHEST, preferred_element_type=jnp.float32)


def normalize(values):
    center = values - jnp.mean(values, axis=-1, keepdims=True)
    inv_std = lax.rsqrt(jnp.mean(center * center, axis=-1, keepdims=True) + epsilon)
    return (center * inv_std, inv_std)


def norm_back(normed, inv_std, upstream):
    mean_up = jnp.mean(upstream, axis=-1, keepdims=True)
    mean_proj = jnp.mean(upstream * normed, axis=-1, keepdims=True)
    return (upstream - mean_up - normed * mean_proj) * inv_std


def local_front(
    pair_input,
    saved_product,
    pair_grad,
    pair_mask,
    w_one,
    w_two,
    w_three,
    w_left,
    w_left_gate,
    w_right,
    w_right_gate,
    w_out,
    w_out_gate,
):
    normed_in, inv_in = normalize(pair_input)
    hidden_one = matmul(normed_in, w_one)
    hidden_two = matmul(normed_in, w_two)
    updated = pair_input + matmul(jax.nn.silu(hidden_one) * hidden_two, w_three)
    normed_mid, inv_mid = normalize(updated)
    left_proj = matmul(normed_mid, w_left)
    left_gate = jax.nn.sigmoid(matmul(normed_mid, w_left_gate))
    right_proj = matmul(normed_mid, w_right)
    right_gate = jax.nn.sigmoid(matmul(normed_mid, w_right_gate))
    left_op = (pair_mask * left_gate * left_proj).astype(jnp.bfloat16)
    right_op = (pair_mask * right_gate * right_proj).astype(jnp.bfloat16)
    normed_out, inv_out = normalize(saved_product)
    out_gate = jax.nn.sigmoid(matmul(normed_mid, w_out_gate))
    gate_term = pair_grad * matmul(normed_out, w_out) * out_gate * (1.0 - out_gate)
    grad_normed = matmul(pair_grad * out_gate, w_out.T)
    grad_product = norm_back(normed_out, inv_out, grad_normed).astype(jnp.bfloat16)
    kept_values = (
        normed_in,
        inv_in,
        hidden_one,
        hidden_two,
        normed_mid,
        inv_mid,
        left_proj,
        left_gate,
        right_proj,
        right_gate,
        gate_term,
    )
    return (grad_product, left_op, right_op, kept_values)


def local_back(
    pair_grad,
    pair_mask,
    kept_values,
    grad_left,
    grad_right,
    w_one,
    w_two,
    w_three,
    w_left,
    w_left_gate,
    w_right,
    w_right_gate,
    w_out_gate,
):
    (
        normed_in,
        inv_in,
        hidden_one,
        hidden_two,
        normed_mid,
        inv_mid,
        left_proj,
        left_gate,
        right_proj,
        right_gate,
        gate_term,
    ) = kept_values
    left_scaled = grad_left * pair_mask * left_gate
    right_scaled = grad_right * pair_mask * right_gate
    grad_mid = matmul(gate_term, w_out_gate.T)
    grad_mid = (
        grad_mid
        + matmul(left_scaled, w_left.T)
        + matmul(left_scaled * left_proj * (1.0 - left_gate), w_left_gate.T)
    )
    grad_mid = (
        grad_mid
        + matmul(right_scaled, w_right.T)
        + matmul(right_scaled * right_proj * (1.0 - right_gate), w_right_gate.T)
    )
    grad_updated = pair_grad + norm_back(normed_mid, inv_mid, grad_mid)
    grad_hidden = matmul(grad_updated, w_three.T)
    sig_one = jax.nn.sigmoid(hidden_one)
    grad_one = grad_hidden * hidden_two * sig_one * (1.0 + hidden_one * (1.0 - sig_one))
    grad_two = grad_hidden * hidden_one * sig_one
    grad_normed_in = matmul(grad_one, w_one.T) + matmul(grad_two, w_two.T)
    return grad_updated + norm_back(normed_in, inv_in, grad_normed_in)


def column_slice(grad_tile, offset, tile_rows):
    return lax.dynamic_slice_in_dim(
        lax.all_gather(grad_tile, "row", axis=0, tiled=True), offset, tile_rows, 1
    )


def operand_fold(left_tile, right_tile, grad_rows, grad_cols):
    left_piece = lax.all_gather(left_tile, "row", axis=0, tiled=True)
    right_piece = lax.all_gather(right_tile, "row", axis=0, tiled=True)
    left_total = jnp.einsum(
        "ijc,jkc->ikc", grad_rows, right_piece, preferred_element_type=jnp.float32
    )
    right_total = jnp.einsum(
        "ijc,ikc->jkc", grad_cols, left_piece, preferred_element_type=jnp.float32
    )
    return (left_total, right_total)


def per_device(
    pair_input,
    saved_product,
    pair_grad,
    token_mask,
    w_one,
    w_two,
    w_three,
    w_left,
    w_left_gate,
    w_right,
    w_right_gate,
    w_out,
    w_out_gate,
):
    tile_rows = pair_input.shape[0]
    tile_cols = pair_input.shape[1]
    row_index = lax.axis_index("row")
    first_row = row_index * tile_rows
    row_mask = lax.dynamic_slice_in_dim(token_mask, first_row, tile_rows).astype(jnp.float32)
    col_mask = lax.dynamic_slice_in_dim(
        token_mask, lax.axis_index(("col", "ch")) * tile_cols, tile_cols
    ).astype(jnp.float32)
    pair_mask = (row_mask[:, None] * col_mask[None, :])[:, :, None]
    grad_product, left_op, right_op, kept_values = local_front(
        pair_input,
        saved_product,
        pair_grad,
        pair_mask,
        w_one,
        w_two,
        w_three,
        w_left,
        w_left_gate,
        w_right,
        w_right_gate,
        w_out,
        w_out_gate,
    )
    grad_tile, left_tile, right_tile = (
        lax.all_to_all(grad_product, "ch", split_axis=2, concat_axis=1, tiled=True),
        lax.all_to_all(left_op, "ch", split_axis=2, concat_axis=1, tiled=True),
        lax.all_to_all(right_op, "ch", split_axis=2, concat_axis=1, tiled=True),
    )
    block_width = grad_tile.shape[1]
    offset = first_row - lax.axis_index("col") * block_width
    root_col = first_row // block_width
    grad_rows = lax.all_gather(grad_tile, "col", axis=1, tiled=True)
    grad_cols = from_root(column_slice(grad_tile, offset, tile_rows), "col", root_col)
    grad_left, grad_right = operand_fold(left_tile, right_tile, grad_rows, grad_cols)
    grad_left, grad_right = (
        lax.all_to_all(grad_left, "ch", split_axis=1, concat_axis=2, tiled=True),
        lax.all_to_all(grad_right, "ch", split_axis=1, concat_axis=2, tiled=True),
    )
    return local_back(
        pair_grad,
        pair_mask,
        kept_values,
        grad_left,
        grad_right,
        w_one,
        w_two,
        w_three,
        w_left,
        w_left_gate,
        w_right,
        w_right_gate,
        w_out_gate,
    )


def solution(mesh):
    in_specs = (
        P(("grp", "row"), ("col", "ch"), None),
        P(("grp", "row"), ("col", "ch"), None),
        P(("grp", "row"), ("col", "ch"), None),
        P("grp"),
        P(),
        P(),
        P(),
        P(),
        P(),
        P(),
        P(),
        P(),
        P(),
    )
    out_specs = P(("grp", "row"), ("col", "ch"), None)
    return jax.shard_map(
        per_device, mesh=mesh, in_specs=in_specs, out_specs=out_specs, check_vma=False
    )
```

profile of v0, /device:TPU:0, one launch (start us, length us, event | category | flops | bytes accessed | tf_op | source)
XLA Modules:
  0.0 181.6 jit_solution(9830218538970233486)
XLA Ops:
  6.5 1.1 reduce_sum.110
  7.7 1.1 multiply_reduce_fusion.4
  8.8 1.6 fusion.29
  10.4 1.8 fusion.32
  12.3 0.8 fusion.77
  13.5 0.4 fusion.8
  14.7 1.1 multiply_convert_fusion
  15.8 0.4 copy.44
  16.2 1.1 reshape.96
  17.4 3.3 %all-to-all-start = ((bf16[2,2,9216]{2,1,0:T(2,128)(2,1)}), bf16[2,2,9216]{2,1,0:T(2,128)(2,1)S(1)}, u32[]{:S(2)}, u32[]{:S(2)}) async-start(bf16[2,2,9216]{2,1,0:T(2,128)(2,1)} %reshape.96), calls=%async_computation | async-start | bytes 147456 | tf_op jit(solution)/shard_map/all_to_all | solution.py:187
  20.7 0.4 fusion.4
  21.5 0.4 fusion.76
  22.1 0.4 copy.47
  22.6 1.1 reshape.98
  23.7 3.3 %all-to-all-start.1 = ((bf16[2,2,9216]{2,1,0:T(2,128)(2,1)}), bf16[2,2,9216]{2,1,0:T(2,128)(2,1)S(1)}, u32[]{:S(2)}, u32[]{:S(2)}) async-start(bf16[2,2,9216]{2,1,0:T(2,128)(2,1)} %reshape.98), calls=%async_computation.1 | async-start | bytes 147456 | tf_op jit(solution)/shard_map/all_to_all | solution.py:185
  27.0 0.6 reshape.97
  27.6 0.4 copy.63
  28.1 35.7 %all_gather.12 = bf16[96,48,64]{2,1,0:T(8,128)(2,1)S(1)} all-gather(bf16[12,48,64]{2,1,0:T(8,128)(2,1)S(1)} %bitcast.103), channel_id=1, replica_groups=mesh['grp'=1,'row'=8,'col'=2,'ch'=2] {'row'}, dimensions={0}, use_global_device_ids=true | all-gather | bytes 663552 | tf_op jit(solution)/shard_map/all_gather | solution.py:135
  63.8 1.4 copy.50
  65.2 0.6 reshape.99
  65.8 0.4 copy.64
  66.2 5.8 %all_gather.13 = bf16[12,96,64]{2,1,0:T(8,128)(2,1)S(1)} all-gather(bf16[12,48,64]{2,1,0:T(8,128)(2,1)S(1)} %bitcast.100), channel_id=1, replica_groups=mesh['grp'=1,'row'=8,'col'=2,'ch'=2] {'col'}, dimensions={1}, use_global_device_ids=true | all-gather | bytes 221184 | tf_op jit(solution)/shard_map/all_gather | solution.py:192
  72.3 0.5 convolution_bitcast_fusion.1
  73.2 0.8 reshape.100
  74.0 3.4 %all-to-all-start.2 = ((f32[2,1,18432]{2,1,0:T(1,128)}), f32[2,1,18432]{2,1,0:T(1,128)S(1)}, u32[]{:S(2)}, u32[]{:S(2)}) async-start(f32[2,1,18432]{2,1,0:T(1,128)} %reshape.100), calls=%async_computation.2 | async-start | bytes 294912 | tf_op jit(solution)/shard_map/all_to_all | solution.py:196
  77.5 34.6 %all_gather.15 = bf16[96,48,64]{2,1,0:T(8,128)(2,1)S(1)} all-gather(bf16[12,48,64]{2,1,0:T(8,128)(2,1)S(1)} %bitcast.101), channel_id=1, replica_groups=mesh['grp'=1,'row'=8,'col'=2,'ch'=2] {'row'}, dimensions={0}, use_global_device_ids=true | all-gather | bytes 663552 | tf_op jit(solution)/shard_map/all_gather | solution.py:129
  112.3 0.5 copy.68
  112.8 0.7 broadcast_select_fusion
  114.0 1.0 fusion.64
  114.9 0.4 copy.55
  115.4 1.1 reshape.102
  116.5 3.3 %all-to-all-start.3 = ((bf16[2,2,9216]{2,1,0:T(2,128)(2,1)}), bf16[2,2,9216]{2,1,0:T(2,128)(2,1)S(1)}, u32[]{:S(2)}, u32[]{:S(2)}) async-start(bf16[2,2,9216]{2,1,0:T(2,128)(2,1)} %reshape.102), calls=%async_computation.3 | async-start | bytes 147456 | tf_op jit(solution)/shard_map/all_to_all | solution.py:186
  119.8 0.5 broadcast.150
  120.4 1.1 reduce
  122.1 0.6 reshape.103
  122.7 0.4 copy.66
  123.1 33.9 %all_gather.14 = bf16[96,48,64]{2,1,0:T(8,128)(2,1)S(1)} all-gather(bf16[12,48,64]{2,1,0:T(8,128)(2,1)S(1)} %bitcast.106), channel_id=1, replica_groups=mesh['grp'=1,'row'=8,'col'=2,'ch'=2] {'row'}, dimensions={0}, use_global_device_ids=true | all-gather | bytes 663552 | tf_op jit(solution)/shard_map/all_gather | solution.py:134
  157.1 1.4 copy.59
  158.4 1.3 convolution_add_fusion.5
  159.8 2.0 %convolution_add_fusion.4 = f32[12,24,128]{2,1,0:T(8,128)} fusion(f32[12,24,128]{2,1,0:T(8,128)S(1)} %convolution_add_fusion.5, f32[12,24,128]{2,1,0:T(8,128)} %copy-done.6, f32[12,24,128]{2,1,0:T(8,128)} %get-tuple-element.15, f32[12,24,128]{2,1,0:T(8,128)S(1)} %all_to_all.76, f32[12,24]{1,0:T(8,128)S(1)} %get-tuple-element.20, f32[128,128]{1,0:T(8,128)} %param.21), kind=kOutput, calls=%fused_computation.18 | convolution fusion | flops 56844288 | bytes 803968 | tf_op jit(solution)/shard_map/dot_general | solution.py:15
  161.7 1.5 convolution_bitcast_fusion
  163.8 4.0 %all_to_all.90 = f32[2,1,18432]{2,1,0:T(1,128)S(1)} all-to-all(f32[2,1,18432]{2,1,0:T(1,128)S(1)} %reshape.104), channel_id=1, replica_groups=mesh['grp'=1,'row'=8,'col'=2,'ch'=2] {'ch'}, dimensions={0} | all-to-all | bytes 294912 | tf_op jit(solution)/shard_map/all_to_all | solution.py:197
  167.8 1.1 reduce.1
  169.9 0.4 fusion.75
  170.6 1.6 fusion.25
  172.2 0.8 fusion.13
  173.0 0.8 fusion.74
  173.9 0.9 multiply_add_fusion
  (128 shorter events, 5.5 us)
Async XLA Ops:
  6.5 2.2 %copy-start = (f32[128,512]{1,0:T(8,128)S(1)}, f32[128,512]{1,0:T(8,128)}, u32[]{:S(2)}) copy-start(f32[128,512]{1,0:T(8,128)} %param.18) | copy-start | bytes 786436
  6.5 5.7 %copy-start.2 = (f32[12,24,128]{2,1,0:T(8,128)S(1)}, f32[12,24,128]{2,1,0:T(8,128)}, u32[]{:S(2)}) copy-start(f32[12,24,128]{2,1,0:T(8,128)} %param.13) | copy-start | bytes 442372
  6.5 3.9 %copy-start.20 = (f32[128,512]{1,0:T(8,128)S(1)}, f32[128,512]{1,0:T(8,128)}, u32[]{:S(2)}) copy-start(f32[128,512]{1,0:T(8,128)} %param.17) | copy-start | bytes 786436
  6.5 5.7 %copy-start.19 = (f32[512,128]{1,0:T(8,128)S(1)}, f32[512,128]{1,0:T(8,128)}, u32[]{:S(2)}) copy-start(f32[512,128]{1,0:T(8,128)} %param.19) | copy-start | bytes 786436
  8.8 1.6 copy-start.32
  10.4 2.6 %copy-start.13 = (f32[12,24,512]{2,1,0:T(8,128)}, f32[12,24,512]{2,1,0:T(8,128)S(1)}, u32[]{:S(2)}) copy-start(f32[12,24,512]{2,1,0:T(8,128)S(1)} %fusion.29) | copy-start | bytes 1769476
  12.2 1.3 copy-start.11
  12.2 0.9 copy-start.41
  12.2 1.3 copy-start.36
  12.2 1.7 copy-start.22
  12.3 2.0 %copy-start.39 = (f32[128,128]{1,0:T(8,128)S(1)}, f32[128,128]{1,0:T(8,128)}, u32[]{:S(2)}) copy-start(f32[128,128]{1,0:T(8,128)} %param.23) | copy-start | bytes 196612
  13.1 1.6 copy-start.26
  13.5 7.2 %copy-start.28 = (f32[12,24]{1,0:T(8,128)}, f32[12,24]{1,0:T(8,128)S(1)}, u32[]{:S(2)}) copy-start(f32[12,24]{1,0:T(8,128)S(1)} %get-tuple-element.19) | copy-start | bytes 3460
  13.9 1.9 %copy-start.6 = (f32[12,24,128]{2,1,0:T(8,128)}, f32[12,24,128]{2,1,0:T(8,128)S(1)}, u32[]{:S(2)}) copy-start(f32[12,24,128]{2,1,0:T(8,128)S(1)} %fusion.8) | copy-start | bytes 442372
  14.3 1.5 copy-start.7
  14.3 6.4 %copy-start.37 = (f32[128,128]{1,0:T(8,128)S(1)}, f32[128,128]{1,0:T(8,128)}, u32[]{:S(2)}) copy-start(f32[128,128]{1,0:T(8,128)} %param.25) | copy-start | bytes 196612
  14.7 1.1 copy-start.9
  14.7 6.4 %copy-start.1 = (f32[12,24,128]{2,1,0:T(8,128)S(1)}, f32[12,24,128]{2,1,0:T(8,128)}, u32[]{:S(2)}) copy-start(f32[12,24,128]{2,1,0:T(8,128)} %param.14) | copy-start | bytes 442372
  14.7 6.7 %copy-start.3 = (f32[12,24,128]{2,1,0:T(8,128)S(1)}, f32[12,24,128]{2,1,0:T(8,128)}, u32[]{:S(2)}) copy-start(f32[12,24,128]{2,1,0:T(8,128)} %param.15) | copy-start | bytes 442372
  14.7 6.7 %copy-start.24 = (f32[128,128]{1,0:T(8,128)S(1)}, f32[128,128]{1,0:T(8,128)}, u32[]{:S(2)}) copy-start(f32[128,128]{1,0:T(8,128)} %param.24) | copy-start | bytes 196612
  17.4 6.3 %all-to-all-start = ((bf16[2,2,9216]{2,1,0:T(2,128)(2,1)}), bf16[2,2,9216]{2,1,0:T(2,128)(2,1)S(1)}, u32[]{:S(2)}, u32[]{:S(2)}) async-start(bf16[2,2,9216]{2,1,0:T(2,128)(2,1)} %reshape.96), calls=%async_computation | async-start | bytes 147456 | tf_op jit(solution)/shard_map/all_to_all | solution.py:187
  21.1 0.8 copy-start.16
  21.2 2.5 %copy-start.30 = (f32[12,24]{1,0:T(8,128)}, f32[12,24]{1,0:T(8,128)S(1)}, u32[]{:S(2)}) copy-start(f32[12,24]{1,0:T(8,128)S(1)} %broadcast_multiply_fusion.9) | copy-start | bytes 3460
  21.4 2.3 %copy-start.34 = (f32[12,24]{1,0:T(8,128)}, f32[12,24]{1,0:T(8,128)S(1)}, u32[]{:S(2)}) copy-start(f32[12,24]{1,0:T(8,128)S(1)} %add_rsqrt_fusion.2) | copy-start | bytes 3460
  23.7 41.5 %all-to-all-start.1 = ((bf16[2,2,9216]{2,1,0:T(2,128)(2,1)}), bf16[2,2,9216]{2,1,0:T(2,128)(2,1)S(1)}, u32[]{:S(2)}, u32[]{:S(2)}) async-start(bf16[2,2,9216]{2,1,0:T(2,128)(2,1)} %reshape.98), calls=%async_computation.1 | async-start | bytes 147456 | tf_op jit(solution)/shard_map/all_to_all | solution.py:185
  74.0 42.5 %all-to-all-start.2 = ((f32[2,1,18432]{2,1,0:T(1,128)}), f32[2,1,18432]{2,1,0:T(1,128)S(1)}, u32[]{:S(2)}, u32[]{:S(2)}) async-start(f32[2,1,18432]{2,1,0:T(1,128)} %reshape.100), calls=%async_computation.2 | async-start | bytes 294912 | tf_op jit(solution)/shard_map/all_to_all | solution.py:196
  77.4 36.1 %copy-start.4 = (f32[12,24,128]{2,1,0:T(8,128)S(1)}, f32[12,24,128]{2,1,0:T(8,128)}, u32[]{:S(2)}) copy-start(f32[12,24,128]{2,1,0:T(8,128)} %param.15) | copy-start | bytes 442372
  77.5 36.1 %copy-start.17 = (f32[12,24,128]{2,1,0:T(8,128)S(1)}, f32[12,24,128]{2,1,0:T(8,128)}, u32[]{:S(2)}) copy-start(f32[12,24,128]{2,1,0:T(8,128)} %copy-done.16) | copy-start | bytes 442372
  77.5 36.1 %copy-start.25 = (f32[128,128]{1,0:T(8,128)S(1)}, f32[128,128]{1,0:T(8,128)}, u32[]{:S(2)}) copy-start(f32[128,128]{1,0:T(8,128)} %param.24) | copy-start | bytes 196612
  77.5 36.1 %copy-start.31 = (f32[12,24]{1,0:T(8,128)S(1)}, f32[12,24]{1,0:T(8,128)}, u32[]{:S(2)}) copy-start(f32[12,24]{1,0:T(8,128)} %copy-done.30) | copy-start | bytes 3460
  77.5 36.1 %copy-start.35 = (f32[12,24]{1,0:T(8,128)S(1)}, f32[12,24]{1,0:T(8,128)}, u32[]{:S(2)}) copy-start(f32[12,24]{1,0:T(8,128)} %copy-done.34) | copy-start | bytes 3460
  77.5 84.2 %all-reduce.2.cloned.1.call-start = ((), (), s32[]{:S(2)}) async-start(), calls=%async_computation.5 | async-start | bytes 524288 | tf_op jit(solution)/shard_map/psum | solution.py:11
  112.1 1.8 %copy-start.38 = (f32[128,128]{1,0:T(8,128)S(1)}, f32[128,128]{1,0:T(8,128)}, u32[]{:S(2)}) copy-start(f32[128,128]{1,0:T(8,128)} %param.25) | copy-start | bytes 196612
  112.2 2.8 %copy-start.18 = (bf16[12,24,128]{2,1,0:T(8,128)(2,1)S(1)}, bf16[12,24,128]{2,1,0:T(8,128)(2,1)}, u32[]{:S(2)}) copy-start(bf16[12,24,128]{2,1,0:T(8,128)(2,1)} %get-tuple-element.11) | copy-start | bytes 221188
  116.5 5.6 %all-to-all-start.3 = ((bf16[2,2,9216]{2,1,0:T(2,128)(2,1)}), bf16[2,2,9216]{2,1,0:T(2,128)(2,1)S(1)}, u32[]{:S(2)}, u32[]{:S(2)}) async-start(bf16[2,2,9216]{2,1,0:T(2,128)(2,1)} %reshape.102), calls=%async_computation.3 | async-start | bytes 147456 | tf_op jit(solution)/shard_map/all_to_all | solution.py:186
  157.1 1.4 copy-start.27
  163.5 6.0 %copy-start.10 = (f32[12,24,128]{2,1,0:T(8,128)S(1)}, f32[12,24,128]{2,1,0:T(8,128)}, u32[]{:S(2)}) copy-start(f32[12,24,128]{2,1,0:T(8,128)} %copy-done.9) | copy-start | bytes 442372
  163.5 5.9 %copy-start.15 = (f32[12,24,128]{2,1,0:T(8,128)S(1)}, f32[12,24,128]{2,1,0:T(8,128)}, u32[]{:S(2)}) copy-start(f32[12,24,128]{2,1,0:T(8,128)} %convolution_add_fusion.4) | copy-start | bytes 442372
  163.6 5.9 %copy-start.23 = (f32[128,128]{1,0:T(8,128)S(1)}, f32[128,128]{1,0:T(8,128)}, u32[]{:S(2)}) copy-start(f32[128,128]{1,0:T(8,128)} %param.22) | copy-start | bytes 196612
  163.8 6.1 %copy-start.8 = (f32[12,24,128]{2,1,0:T(8,128)S(1)}, f32[12,24,128]{2,1,0:T(8,128)}, u32[]{:S(2)}) copy-start(f32[12,24,128]{2,1,0:T(8,128)} %copy-done.7) | copy-start | bytes 442372
  163.8 6.1 %copy-start.29 = (f32[12,24]{1,0:T(8,128)S(1)}, f32[12,24]{1,0:T(8,128)}, u32[]{:S(2)}) copy-start(f32[12,24]{1,0:T(8,128)} %copy-done.28) | copy-start | bytes 3460
  163.8 6.1 %copy-start.40 = (f32[128,128]{1,0:T(8,128)S(1)}, f32[128,128]{1,0:T(8,128)}, u32[]{:S(2)}) copy-start(f32[128,128]{1,0:T(8,128)} %param.23) | copy-start | bytes 196612
  168.8 1.6 copy-start.5
  169.5 2.7 %copy-start.12 = (f32[12,24,512]{2,1,0:T(8,128)S(1)}, f32[12,24,512]{2,1,0:T(8,128)}, u32[]{:S(2)}) copy-start(f32[12,24,512]{2,1,0:T(8,128)} %copy-done.11) | copy-start | bytes 1769476
  169.5 2.7 %copy-start.14 = (f32[12,24,512]{2,1,0:T(8,128)S(1)}, f32[12,24,512]{2,1,0:T(8,128)}, u32[]{:S(2)}) copy-start(f32[12,24,512]{2,1,0:T(8,128)} %copy-done.13) | copy-start | bytes 1769476
  169.5 2.7 %copy-start.21 = (f32[128,512]{1,0:T(8,128)S(1)}, f32[128,512]{1,0:T(8,128)}, u32[]{:S(2)}) copy-start(f32[128,512]{1,0:T(8,128)} %param.17) | copy-start | bytes 786436
  172.2 0.8 copy-start.33
Sparse Core Ops, SparseCore 0:
  113.7 23.4 all-reduce.1
where the time goes:
time: 182 us
  blocking collectives  114 us (63%)
  matrix products  17.5 us (10%)
  local copies, waits for them, and re-layouts  15.2 us (8%)
  between operations  14.4 us (8%)
  starting transfers between devices  13.4 us (7%)
  other arithmetic  7.11 us (4%)
    all_gather x1, blocking collectives, operand_fold(): right_piece = lax.all_gather(right_tile, 'row', axis=0, tiled=True)  35.7 us
    all_gather x1, blocking collectives, column_slice(): lax.all_gather(grad_tile, 'row', axis=0, tiled=True)  34.6 us
    all_gather x1, blocking collectives, operand_fold(): left_piece = lax.all_gather(left_tile, 'row', axis=0, tiled=True)  33.9 us
    dot_general x18, matrix products, matmul(): jnp.dot(left, right, precision=lax.Precision.HIGHEST, preferred_element_t...  15.5 us
    unnamed x95, local copies, waits for them, and re-layouts  7.42 us
    all_gather x1, blocking collectives, per_device(): grad_rows = lax.all_gather(grad_tile, 'col', axis=1, tiled=True)  5.82 us
    all_to_all x1, blocking collectives, per_device(): lax.all_to_all(grad_right, 'ch', split_axis=1, concat_axis=2, tiled=True)  3.96 us
  transfers between devices with their start and end apart: 5, of which 0 were waited for; matrix products, arithmetic and copies ran while one was open for 9% of the time, Pallas kernels for 0%

commit v1 on v0

v1 whole, which is shorter than its diff:
```python
import functools

import jax
import jax.numpy as jnp
from jax import lax
from jax.experimental import pallas as pl
from jax.experimental.pallas import tpu as pltpu
from jax.sharding import PartitionSpec as P

epsilon = 1e-05
f32 = jnp.float32
bf16 = jnp.bfloat16
MESH = pl.DeviceIdType.MESH


def split(values):
    high = values.astype(bf16)
    return high, (values - high.astype(f32)).astype(bf16)


def matmul(values, high_ref, low_ref, cols=None, transposed=False):
    dims = (((1,), (1 if transposed else 0,)), ((), ()))
    high, low = split(values)
    w_high = high_ref[...] if cols is None else high_ref[:, cols[0] : cols[1]]
    w_low = low_ref[...] if cols is None else low_ref[:, cols[0] : cols[1]]
    dot = functools.partial(lax.dot_general, dimension_numbers=dims, preferred_element_type=f32)
    return dot(high, w_high) + (dot(low, w_high) + dot(high, w_low))


def sigmoid(values):
    return 0.5 * jnp.tanh(0.5 * values) + 0.5


def normalize(values):
    center = values - jnp.mean(values, axis=-1, keepdims=True)
    inv_std = lax.rsqrt(jnp.mean(center * center, axis=-1, keepdims=True) + epsilon)
    return (center * inv_std, inv_std)


def norm_back(normed, inv_std, upstream):
    mean_up = jnp.mean(upstream, axis=-1, keepdims=True)
    mean_proj = jnp.mean(upstream * normed, axis=-1, keepdims=True)
    return (upstream - mean_up - normed * mean_proj) * inv_std


def kernel(
    sizes,
    x_ref,
    s_ref,
    g_ref,
    mask_ref,
    w1_ref,
    w2_ref,
    w3_ref,
    wl_ref,
    wlg_ref,
    wr_ref,
    wrg_ref,
    wo_ref,
    wog_ref,
    out_ref,
    w12h,
    w12l,
    w3h,
    w3l,
    w5h,
    w5l,
    woh,
    wol,
    h1s,
    h2s,
    nms,
    ims,
    lgm,
    lq,
    rgm,
    rq,
    gts,
    left32,
    right32,
    gp32,
    accl,
    accr,
    gp_all,
    right_all,
    part_y,
    got_y,
    part_z,
    got_z,
    ag_send,
    ag_recv,
    fw_send,
    gp_send,
    gp_recv,
    ys_send,
    ys_recv,
    zs_send,
    zs_recv,
):
    rows, pairs, tr, tc, tokens, n_col, n_ch, chunk, ktile = sizes
    n_k = n_col * n_ch
    n_z = rows // 2
    hid = w1_ref.shape[1]
    row = lax.axis_index("row")
    my_z, my_y = row // 2, row % 2
    col, ch = lax.axis_index("col"), lax.axis_index("ch")
    my_k = col * n_ch + ch
    y_peer = my_z * 2 + (1 - my_y)
    z_steps = range(1, n_z)
    k_steps = range(1, n_k)

    def z_at(step):
        return lax.rem(my_z + step, n_z)

    def k_peer(step):
        other = lax.rem(my_k + step, n_k)
        return {"col": other // n_ch, "ch": other % n_ch}

    barrier = pltpu.get_barrier_semaphore()
    for step in z_steps:
        pl.semaphore_signal(barrier, inc=1, device_id={"row": z_at(step) * 2 + my_y}, device_id_type=MESH)
    pl.semaphore_signal(barrier, inc=1, device_id={"row": y_peer}, device_id_type=MESH)
    for step in k_steps:
        pl.semaphore_signal(barrier, inc=1, device_id=k_peer(step), device_id_type=MESH)

    def put(high_ref, low_ref, at, source):
        high, low = split(source[...])
        high_ref[:, at : at + high.shape[1]] = high
        low_ref[:, at : at + high.shape[1]] = low

    put(w12h, w12l, 0, w1_ref)
    put(w12h, w12l, hid, w2_ref)
    put(w3h, w3l, 0, w3_ref)
    for place, source in enumerate((wl_ref, wlg_ref, wr_ref, wrg_ref, wog_ref)):
        put(w5h, w5l, place * 128, source)
    put(woh, wol, 0, wo_ref)

    token = lax.broadcasted_iota(jnp.int32, (tc, tokens), 1)
    spot = lax.broadcasted_iota(jnp.int32, (tc, tokens), 0)
    mask = mask_ref[...].astype(f32)
    col_mask = jnp.sum(
        jnp.where(token == spot + my_k * tc, jnp.broadcast_to(mask, (tc, tokens)), 0.0), axis=1, keepdims=True
    )
    col_mask = jnp.concatenate([jnp.broadcast_to(col_mask, (tc, 128))] * (chunk // tc), axis=0)

    def front(step, carry):
        base = pl.multiple_of(step * chunk, chunk)
        here = pl.ds(base, chunk)
        token = lax.broadcasted_iota(jnp.int32, (chunk, tokens), 1)
        spot = lax.broadcasted_iota(jnp.int32, (chunk, tokens), 0) + base
        ahead = spot - (token - row * tr) * tc
        row_mask = jnp.sum(
            jnp.where((ahead >= 0) & (ahead < tc), jnp.broadcast_to(mask, (chunk, tokens)), 0.0), axis=1, keepdims=True
        )
        pair_mask = col_mask * row_mask
        pair_input = x_ref[here, :]
        normed_in, _ = normalize(pair_input)
        hidden = matmul(normed_in, w12h, w12l)
        hidden_one, hidden_two = hidden[:, :hid], hidden[:, hid:]
        h1s[here, :] = hidden_one
        h2s[here, :] = hidden_two
        act = hidden_one * sigmoid(hidden_one) * hidden_two
        updated = pair_input + matmul(act, w3h, w3l)
        normed_mid, inv_mid = normalize(updated)
        nms[here, :] = normed_mid
        ims[here, :] = jnp.broadcast_to(inv_mid, (chunk, 128))
        proj = matmul(normed_mid, w5h, w5l)
        right_proj, right_gate = proj[:, 256:384], sigmoid(proj[:, 384:512])
        masked = pair_mask * right_gate
        rgm[here, :] = masked
        rq[here, :] = right_proj * (1.0 - right_gate)
        right_op = (masked * right_proj).astype(bf16)
        right_all[row, here, :] = right_op
        left_proj, left_gate = proj[:, :128], sigmoid(proj[:, 128:256])
        masked = pair_mask * left_gate
        lgm[here, :] = masked
        lq[here, :] = left_proj * (1.0 - left_gate)
        left32[here, :] = (masked * left_proj).astype(bf16).astype(f32)
        out_gate = sigmoid(proj[:, 512:640])
        pair_grad = g_ref[here, :]
        normed_out, inv_out = normalize(s_ref[here, :])
        gts[here, :] = pair_grad * matmul(normed_out, woh, wol) * out_gate * (1.0 - out_gate)
        grad_normed = matmul(pair_grad * out_gate, woh, wol, transposed=True)
        gp_all[my_k, here, :] = norm_back(normed_out, inv_out, grad_normed).astype(bf16)
        return carry

    lax.fori_loop(0, pairs // chunk, front, 0)
    pl.semaphore_wait(barrier, n_z + n_k - 1)

    def right_copy(slot, sem, target):
        return pltpu.make_async_remote_copy(
            src_ref=right_all.at[slot],
            dst_ref=right_all.at[slot],
            send_sem=sem,
            recv_sem=ag_recv.at[slot],
            device_id={"row": target},
            device_id_type=MESH,
        )

    sends = []

    def start(copy):
        copy.start()
        sends.append(copy)

    for step in k_steps:
        start(
            pltpu.make_async_remote_copy(
                src_ref=gp_all.at[my_k],
                dst_ref=gp_all.at[my_k],
                send_sem=gp_send.at[step],
                recv_sem=gp_recv.at[my_k],
                device_id=k_peer(step),
                device_id_type=MESH,
            )
        )
    for step in z_steps:
        start(right_copy(row, ag_send.at[step], z_at(step) * 2 + my_y))
    start(right_copy(row, ag_send.at[0], y_peer))

    def widen(slot):
        gp32[slot] = gp_all[slot].astype(f32)

    widen(my_k)
    for step in k_steps:
        other = lax.rem(my_k + step, n_k)
        pltpu.make_async_remote_copy(
            src_ref=gp_all.at[other],
            dst_ref=gp_all.at[other],
            send_sem=gp_send.at[step],
            recv_sem=gp_recv.at[other],
            device_id=k_peer(step),
            device_id_type=MESH,
        ).wait_recv()
        widen(other)

    def block_rows(owner):
        return (owner * tr) // tc, (owner * tr) % tc

    def partial_right(owner, k_base):
        slot, offset = block_rows(owner)

        def body(i, acc):
            tile = left32[pl.ds(pl.multiple_of(i * tc + k_base, 8), ktile), :]
            return tuple(
                acc[j] + gp32[slot, pl.ds(i * tc + offset + j, 1), :] * tile for j in range(tr)
            )

        return lax.fori_loop(0, tr, body, (jnp.zeros((ktile, 128), f32),) * tr)

    k_bases = range(0, tc, ktile)

    for step in list(z_steps) + [0]:
        z_to = z_at(step)
        for k_base in k_bases:
            acc = partial_right(z_to * 2 + (1 - my_y), k_base)
            for j in range(tr):
                part_y[z_to, pl.ds(j * tc + k_base, ktile), :] = acc[j].astype(bf16)
        start(
            pltpu.make_async_remote_copy(
                src_ref=part_y.at[z_to],
                dst_ref=got_y.at[z_to],
                send_sem=ys_send.at[z_to],
                recv_sem=ys_recv.at[z_to],
                device_id={"row": y_peer},
                device_id_type=MESH,
            )
        )

    for step in z_steps:
        source = lax.rem(my_z + n_z - step, n_z) * 2 + my_y
        right_copy(source, fw_send.at[step], y_peer).wait_recv()
        start(right_copy(source, fw_send.at[step], y_peer))

    def wait_y(z_to):
        pltpu.make_async_remote_copy(
            src_ref=part_y.at[z_to],
            dst_ref=got_y.at[z_to],
            send_sem=ys_send.at[z_to],
            recv_sem=ys_recv.at[z_to],
            device_id={"row": y_peer},
            device_id_type=MESH,
        ).wait_recv()

    def z_copy(source_z, target_z, step):
        return pltpu.make_async_remote_copy(
            src_ref=part_z.at[target_z],
            dst_ref=got_z.at[source_z],
            send_sem=zs_send.at[step],
            recv_sem=zs_recv.at[source_z],
            device_id={"row": target_z * 2 + my_y},
            device_id_type=MESH,
        )

    for step in z_steps:
        z_to = z_at(step)
        for place, k_base in enumerate(k_bases):
            acc = partial_right(z_to * 2 + my_y, k_base)
            if place == 0:
                wait_y(z_to)
            for j in range(tr):
                here = pl.ds(j * tc + k_base, ktile)
                part_z[z_to, here, :] = (acc[j] + got_y[z_to, here, :].astype(f32)).astype(bf16)
        start(z_copy(my_z, z_to, step))

    for k_base in k_bases:
        acc = partial_right(row, k_base)
        for j in range(tr):
            accr[pl.ds(j * tc + k_base, ktile), :] = acc[j]
    wait_y(my_z)
    accr[...] += got_y[my_z].astype(f32)

    def middle(step, carry):
        here = pl.ds(pl.multiple_of(step * 48, 48), 48)
        hidden_one, hidden_two = h1s[here, :], h2s[here, :]
        sig_one = sigmoid(hidden_one)
        h1s[here, :] = hidden_two * sig_one * (1.0 + hidden_one * (1.0 - sig_one))
        h2s[here, :] = hidden_one * sig_one
        return carry

    lax.fori_loop(0, pairs // 48, middle, 0)

    def fold_left(owner, first):
        slot, offset = block_rows(owner)
        right32[...] = right_all[owner].astype(f32)
        for k_base in k_bases:

            def body(j, acc):
                tile = right32[pl.ds(pl.multiple_of(j * tc + k_base, 8), ktile), :]
                return tuple(
                    acc[i] + gp32[slot, pl.ds(i * tc + offset + j, 1), :] * tile for i in range(tr)
                )

            begin = tuple(
                jnp.zeros((ktile, 128), f32) if first else accl[pl.ds(i * tc + k_base, ktile), :] for i in range(tr)
            )
            acc = lax.fori_loop(0, tr, body, begin)
            for i in range(tr):
                accl[pl.ds(i * tc + k_base, ktile), :] = acc[i]

    fold_left(row, True)
    for step in z_steps:
        fold_left(lax.rem(my_z + n_z - step, n_z) * 2 + my_y, False)
    for step in range(n_z):
        source = lax.rem(my_z + n_z - step, n_z) * 2 + (1 - my_y)
        right_copy(source, ag_send.at[0], y_peer).wait_recv()
        fold_left(source, False)

    for step in z_steps:
        source = lax.rem(my_z + n_z - step, n_z)
        z_copy(source, z_at(step), step).wait_recv()
        accr[...] += got_z[source].astype(f32)

    def back(step, carry):
        here = pl.ds(pl.multiple_of(step * chunk, chunk), chunk)
        left_scaled = accl[here, :] * lgm[here, :]
        right_scaled = accr[here, :] * rgm[here, :]
        wide = jnp.concatenate(
            [left_scaled, left_scaled * lq[here, :], right_scaled, right_scaled * rq[here, :], gts[here, :]], axis=1
        )
        grad_mid = matmul(wide, w5h, w5l, transposed=True)
        grad_updated = g_ref[here, :] + norm_back(nms[here, :], ims[here, :], grad_mid)
        grad_hidden = matmul(grad_updated, w3h, w3l, transposed=True)
        both = jnp.concatenate([grad_hidden * h1s[here, :], grad_hidden * h2s[here, :]], axis=1)
        grad_normed_in = matmul(both, w12h, w12l, transposed=True)
        normed_in, inv_in = normalize(x_ref[here, :])
        out_ref[here, :] = grad_updated + norm_back(normed_in, inv_in, grad_normed_in)
        return carry

    lax.fori_loop(0, pairs // chunk, back, 0)
    for copy in sends:
        copy.wait_send()


def per_device(mesh, pair_input, saved_product, pair_grad, token_mask, *weights):
    rows = mesh.shape["row"]
    n_col, n_ch = mesh.shape["col"], mesh.shape["ch"]
    tr, tc, width = pair_input.shape
    pairs = tr * tc
    tokens = token_mask.shape[0]
    hid = weights[0].shape[1]
    chunk = pairs // (pairs // (6 * 24)) if pairs % 144 == 0 else pairs
    ktile = 24 if tc % 24 == 0 else tc
    n_k, n_z = n_col * n_ch, rows // 2
    flat = [array.reshape(pairs, width) for array in (pair_input, saved_product, pair_grad)]
    vmem = pltpu.VMEM
    dma = pltpu.SemaphoreType.DMA
    tile32 = vmem((pairs, width), f32)
    sizes = (rows, pairs, tr, tc, tokens, n_col, n_ch, chunk, ktile)
    out = pl.pallas_call(
        functools.partial(kernel, sizes),
        out_shape=jax.ShapeDtypeStruct((pairs, width), f32),
        in_specs=[pl.BlockSpec(memory_space=vmem)] * 13,
        out_specs=pl.BlockSpec(memory_space=vmem),
        scratch_shapes=[
            vmem((width, 2 * hid), bf16),
            vmem((width, 2 * hid), bf16),
            vmem((hid, width), bf16),
            vmem((hid, width), bf16),
            vmem((width, 5 * width), bf16),
            vmem((width, 5 * width), bf16),
            vmem((width, width), bf16),
            vmem((width, width), bf16),
            vmem((pairs, hid), f32),
            vmem((pairs, hid), f32),
            *([tile32] * 9),
            vmem((n_k, pairs, width), f32),
            tile32,
            tile32,
            vmem((n_k, pairs, width), bf16),
            vmem((rows, pairs, width), bf16),
            *([vmem((n_z, pairs, width), bf16)] * 4),
            dma((n_z,)),
            dma((rows,)),
            dma((n_z,)),
            dma((n_k,)),
            dma((n_k,)),
            *([dma((n_z,))] * 4),
        ],
        compiler_params=pltpu.CompilerParams(
            collective_id=0, has_side_effects=True, vmem_limit_bytes=56 * 1024 * 1024
        ),
    )(*flat, token_mask.reshape(1, tokens), *weights)
    return out.reshape(tr, tc, width)


def solution(mesh):
    tile = P(("grp", "row"), ("col", "ch"), None)
    in_specs = (tile, tile, tile, P("grp")) + (P(),) * 9
    return jax.shard_map(
        functools.partial(per_device, mesh), mesh=mesh, in_specs=in_specs, out_specs=tile, check_vma=False
    )
```

time: 182 us -> 30.9 us (0.17)
  blocking collectives: 114 us -> 0 us
  Pallas kernels: 0 us -> 29.1 us
  matrix products: 17.5 us -> 0 us
  between operations: 14.4 us -> 0.01 us
  local copies, waits for them, and re-layouts: 15.2 us -> 1.58 us
  starting transfers between devices: 13.4 us -> 0 us
  other arithmetic: 7.11 us -> 0 us
    all_gather x4 -> x0, blocking collectives: 110 us -> none  [the longest x1 35.7 us: operand_fold(): right_piece = lax.all_gather(right_tile, 'row', axis=0, tiled=True)]
    pallas_call x0 -> x1, Pallas kernels: none -> 29.1 us  [per_device(): pl.pallas_call(functools.partial(kernel, sizes), out_shape=jax.ShapeDtype...]
    dot_general x20 -> x0, matrix products: 17.5 us -> none  [the longest x18 15.5 us: matmul(): jnp.dot(left, right, precision=lax.Precision.HIGHEST, preferred_element_t...]
    all_to_all x4 -> x0, starting transfers between devices: 13.4 us -> none  [the longest x1 3.42 us: per_device(): lax.all_to_all(grad_left, 'ch', split_axis=1, concat_axis=2, tiled=True)]
    unnamed x95 -> x1, local copies, waits for them, and re-layouts: 7.42 us -> 1.58 us
    all_to_all x1 -> x0, blocking collectives: 3.96 us -> none  [per_device(): lax.all_to_all(grad_right, 'ch', split_axis=1, concat_axis=2, tiled=True)]
    all_gather x3 -> x0, local copies, waits for them, and re-layouts: 2.96 us -> none  [the longest x1 1.35 us: operand_fold(): left_piece = lax.all_gather(left_tile, 'row', axis=0, tiled=True)]
    reduce_sum x5 -> x0, other arithmetic: 2.68 us -> none  [the longest x3 1.47 us: normalize(): jnp.mean(center * center, axis=-1, keepdims=True) + epsilon]
  transfers between devices with their start and end apart: 5 -> 0, of which waited for: 0 -> 0; matrix products, arithmetic and copies ran while one was open for 9% -> 0% of each run, Pallas kernels for 0% -> 0%
where the time goes in v1:
time: 30.9 us; the launch traced here: 30.7 us
  Pallas kernels  29.1 us (94%)
  local copies, waits for them, and re-layouts  1.58 us (5%)
    pallas_call x1, Pallas kernels, per_device(): pl.pallas_call(functools.partial(kernel, sizes), out_shape=jax.ShapeDtype...  29.1 us
    unnamed x1, local copies, waits for them, and re-layouts  1.58 us

profile of v1, /device:TPU:0, one launch (start us, length us, event | category | flops | bytes accessed | tf_op | source)
XLA Modules:
  0.0 30.7 jit_solution(13043683131513578493)
XLA Ops:
  0.0 29.1 %shard_map.127 = f32[288,128]{1,0:T(8,128)} custom-call(f32[288,128]{1,0:T(8,128)} %bitcast.6, f32[288,128]{1,0:T(8,128)} %bitcast.7, f32[288,128]{1,0:T(8,128)} %bitcast.8, s32[1,96]{1,0:T(1,128)} %bitcast.9, f32[128,512]{1,0:T(8,128)} %w1_ref.1, f32[128,512]{1,0:T(8,128)} %w2_ref.1, f32[512,128]{1,0:T(8,128)} %w3_ref.1, f32[128,128]{1,0:T(8,128)} %wl_ref.1, ...), custom_call_target="tpu_custom_call" | custom-call | tf_op jit(solution)/shard_map/pallas_call | solution.py:390
  29.1 1.6 %copy.15 = f32[12,24,128]{2,1,0:T(8,128)} copy(f32[12,24,128]{2,1,0:T(8,128)} %bitcast.5) | data formatting | bytes 294912

commit v2 on v1

v2 whole, which is shorter than its diff:
```python
import functools

import jax
import jax.numpy as jnp
from jax import lax
from jax.experimental import pallas as pl
from jax.experimental.pallas import tpu as pltpu
from jax.sharding import PartitionSpec as P

epsilon = 1e-05
f32 = jnp.float32
bf16 = jnp.bfloat16
MESH = pl.DeviceIdType.MESH


def split(values):
    high = values.astype(bf16)
    return high, (values - high.astype(f32)).astype(bf16)


def matmul(values, high_ref, low_ref, cols=None, transposed=False, parts=3):
    dims = (((1,), (1 if transposed else 0,)), ((), ()))
    high, low = split(values)
    w_high = high_ref[...] if cols is None else high_ref[:, cols[0] : cols[1]]
    w_low = low_ref[...] if cols is None else low_ref[:, cols[0] : cols[1]]
    dot = functools.partial(lax.dot_general, dimension_numbers=dims, preferred_element_type=f32)
    if parts == 2:
        return dot(high, w_high) + dot(low, w_high)
    return dot(high, w_high) + (dot(low, w_high) + dot(high, w_low))


def sigmoid(values):
    return 0.5 * jnp.tanh(0.5 * values) + 0.5


def normalize(values):
    center = values - jnp.mean(values, axis=-1, keepdims=True)
    inv_std = lax.rsqrt(jnp.mean(center * center, axis=-1, keepdims=True) + epsilon)
    return (center * inv_std, inv_std)


def norm_back(normed, inv_std, upstream):
    mean_up = jnp.mean(upstream, axis=-1, keepdims=True)
    mean_proj = jnp.mean(upstream * normed, axis=-1, keepdims=True)
    return (upstream - mean_up - normed * mean_proj) * inv_std


def kernel(
    sizes,
    x_in,
    s_in,
    g_in,
    mask_in,
    w1_in,
    w2_in,
    w3_in,
    wl_in,
    wlg_in,
    wr_in,
    wrg_in,
    wo_in,
    wog_in,
    out_ref,
    w12h,
    w12l,
    w3h,
    w3l,
    w5h,
    w5l,
    woh,
    wol,
    h1s,
    h2s,
    nms,
    ims,
    lgm,
    lq,
    rgm,
    rq,
    gts,
    left32,
    masks,
    right32,
    gp32,
    accl,
    accr,
    accr_all,
    gp_all,
    right_all,
    part_y,
    got_y,
    part_z,
    got_z,
    ag_send,
    ag_recv,
    fw_send,
    gp_send,
    gp_recv,
    ys_send,
    ys_recv,
    zs_send,
    zs_recv,
    in_sem,
    x_ref,
    s_ref,
    g_ref,
    mask_ref,
    w1_ref,
    w2_ref,
    w3_ref,
    wl_ref,
    wlg_ref,
    wr_ref,
    wrg_ref,
    wo_ref,
    wog_ref,
):
    rows, pairs, tr, tc, tokens, n_col, n_ch, chunk, ktile = sizes
    n_k = n_col * n_ch
    n_z = rows // 2
    hid = w1_in.shape[1]
    row = lax.axis_index("row")
    my_z, my_y = row // 2, row % 2
    col, ch = lax.axis_index("col"), lax.axis_index("ch")
    my_k = col * n_ch + ch
    y_peer = my_z * 2 + (1 - my_y)

    places = [(dcol, dch) for dcol in range(n_col) for dch in range(n_ch)]

    def k_place(place):
        return {"col": lax.rem(col + place[0], n_col), "ch": lax.rem(ch + place[1], n_ch)}

    def k_slot(place):
        spot = k_place(place)
        return spot["col"] * n_ch + spot["ch"]

    def z_valid(delta):
        return (my_z + delta >= 0) & (my_z + delta < n_z)

    def z_row(delta):
        return (my_z + delta) * 2 + my_y

    barrier = pltpu.get_barrier_semaphore()
    for delta in [sign * far for far in range(1, n_z) for sign in (1, -1)]:

        @pl.when(z_valid(delta))
        def _():
            pl.semaphore_signal(barrier, inc=1, device_id={"row": z_row(delta)}, device_id_type=MESH)

    pl.semaphore_signal(barrier, inc=1, device_id={"row": y_peer}, device_id_type=MESH)
    for place in places[1:]:
        pl.semaphore_signal(barrier, inc=1, device_id=k_place(place), device_id_type=MESH)

    inputs = []
    for source, target in (
        (x_in, x_ref),
        (w1_in, w1_ref),
        (w2_in, w2_ref),
        (mask_in, mask_ref),
        (w3_in, w3_ref),
        (wr_in, wr_ref),
        (wrg_in, wrg_ref),
        (wog_in, wog_ref),
        (wo_in, wo_ref),
        (s_in, s_ref),
        (g_in, g_ref),
        (wl_in, wl_ref),
        (wlg_in, wlg_ref),
    ):
        copy = pltpu.make_async_copy(source, target, in_sem.at[len(inputs)])
        copy.start()
        inputs.append(copy)
    def loaded(count):
        for _ in range(count):
            inputs.pop(0).wait()

    def put(high_ref, low_ref, at, source):
        high, low = split(source[...])
        high_ref[:, at : at + high.shape[1]] = high
        low_ref[:, at : at + high.shape[1]] = low

    loaded(7)
    put(w12h, w12l, 0, w1_ref)
    put(w12h, w12l, hid, w2_ref)
    put(w3h, w3l, 0, w3_ref)
    put(w5h, w5l, 256, wr_ref)
    put(w5h, w5l, 384, wrg_ref)

    token = lax.broadcasted_iota(jnp.int32, (tc, tokens), 1)
    spot = lax.broadcasted_iota(jnp.int32, (tc, tokens), 0)
    mask = mask_ref[...].astype(f32)
    col_mask = jnp.sum(
        jnp.where(token == spot + my_k * tc, jnp.broadcast_to(mask, (tc, tokens)), 0.0), axis=1, keepdims=True
    )
    col_mask = jnp.concatenate([jnp.broadcast_to(col_mask, (tc, 128))] * (chunk // tc), axis=0)

    def front(step, carry):
        base = pl.multiple_of(step * chunk, chunk)
        here = pl.ds(base, chunk)
        token = lax.broadcasted_iota(jnp.int32, (chunk, tokens), 1)
        spot = lax.broadcasted_iota(jnp.int32, (chunk, tokens), 0) + base
        ahead = spot - (token - row * tr) * tc
        row_mask = jnp.sum(
            jnp.where((ahead >= 0) & (ahead < tc), jnp.broadcast_to(mask, (chunk, tokens)), 0.0), axis=1, keepdims=True
        )
        pair_mask = col_mask * row_mask
        pair_input = x_ref[here, :]
        normed_in, _ = normalize(pair_input)
        hidden = matmul(normed_in, w12h, w12l)
        hidden_one, hidden_two = hidden[:, :hid], hidden[:, hid:]
        h1s[here, :] = hidden_one
        h2s[here, :] = hidden_two
        act = hidden_one * sigmoid(hidden_one) * hidden_two
        updated = pair_input + matmul(act, w3h, w3l)
        normed_mid, inv_mid = normalize(updated)
        nms[here, :] = normed_mid
        ims[here, :] = jnp.broadcast_to(inv_mid, (chunk, 128))
        proj = matmul(normed_mid, w5h, w5l, cols=(256, 512))
        right_proj, right_gate = proj[:, :128], sigmoid(proj[:, 128:256])
        masks[here, :] = pair_mask
        masked = pair_mask * right_gate
        rgm[here, :] = masked
        rq[here, :] = right_proj * (1.0 - right_gate)
        right_op = (masked * right_proj).astype(bf16)
        right_all[row, here, :] = right_op
        return carry

    lax.fori_loop(0, pairs // chunk, front, 0)
    pl.semaphore_wait(barrier, n_k + n_z - 1)

    def right_copy(slot, sem, target):
        return pltpu.make_async_remote_copy(
            src_ref=right_all.at[slot],
            dst_ref=right_all.at[slot],
            send_sem=sem,
            recv_sem=ag_recv.at[slot],
            device_id={"row": target},
            device_id_type=MESH,
        )

    sends = []

    def start(copy):
        copy.start()
        sends.append(copy)

    def start_if(cond, copy):
        pl.when(cond)(copy.start)
        held.append((cond, copy))

    held = []

    def right_send(delta):
        sem = ag_send.at[2 * abs(delta) - 1 + (delta < 0)]
        start_if(z_valid(delta), right_copy(row, sem, z_row(delta)))

    def gp_copy(place, slot):
        return pltpu.make_async_remote_copy(
            src_ref=gp_all.at[slot],
            dst_ref=gp_all.at[slot],
            send_sem=gp_send.at[places.index(place)],
            recv_sem=gp_recv.at[slot],
            device_id=k_place(place),
            device_id_type=MESH,
        )

    for far in range(1, n_z):
        right_send(far)
        right_send(-far)
    start(right_copy(row, ag_send.at[0], y_peer))

    loaded(6)
    put(w5h, w5l, 512, wog_ref)
    put(woh, wol, 0, wo_ref)
    put(w5h, w5l, 0, wl_ref)
    put(w5h, w5l, 128, wlg_ref)

    def gates(step, carry):
        here = pl.ds(pl.multiple_of(step * chunk, chunk), chunk)
        out_gate = sigmoid(matmul(nms[here, :], w5h, w5l, cols=(512, 640)))
        pair_grad = g_ref[here, :]
        normed_out, inv_out = normalize(s_ref[here, :])
        grad_normed = matmul(pair_grad * out_gate, woh, wol, transposed=True)
        gp_all[my_k, here, :] = norm_back(normed_out, inv_out, grad_normed).astype(bf16)
        gts[here, :] = pair_grad * out_gate * (1.0 - out_gate)
        return carry

    lax.fori_loop(0, pairs // chunk, gates, 0)
    for place in places[::-1][:-1]:
        start(gp_copy(place, my_k))

    def lefts(step, carry):
        here = pl.ds(pl.multiple_of(step * chunk, chunk), chunk)
        proj = matmul(nms[here, :], w5h, w5l, cols=(0, 256))
        left_proj, left_gate = proj[:, :128], sigmoid(proj[:, 128:256])
        masked = masks[here, :] * left_gate
        lgm[here, :] = masked
        lq[here, :] = left_proj * (1.0 - left_gate)
        left32[here, :] = (masked * left_proj).astype(bf16).astype(f32)
        return carry

    lax.fori_loop(0, pairs // chunk, lefts, 0)

    def widen(slot):
        gp32[slot] = gp_all[slot].astype(f32)

    def arrive(place):
        slot = k_slot(place)
        gp_copy(place, slot).wait_recv()
        widen(slot)

    widen(my_k)

    def block_rows(owner):
        return (owner * tr) // tc, (owner * tr) % tc

    def partial_right(owner, k_base):
        slot, offset = block_rows(owner)

        def body(i, acc):
            tile = left32[pl.ds(pl.multiple_of(i * tc + k_base, 8), ktile), :]
            return tuple(
                acc[j] + gp32[slot, pl.ds(i * tc + offset + j, 1), :] * tile for j in range(tr)
            )

        return lax.fori_loop(0, tr, body, (jnp.zeros((ktile, 128), f32),) * tr)

    k_bases = range(0, tc, ktile)

    per_slot = n_z // n_k

    def to_y(place):
        for q in range(per_slot):
            z_to = k_slot(place) * per_slot + q
            for k_base in k_bases:
                acc = partial_right(z_to * 2 + (1 - my_y), k_base)
                for j in range(tr):
                    part_y[z_to, pl.ds(j * tc + k_base, ktile), :] = acc[j].astype(bf16)
            start(
                pltpu.make_async_remote_copy(
                    src_ref=part_y.at[z_to],
                    dst_ref=got_y.at[z_to],
                    send_sem=ys_send.at[z_to],
                    recv_sem=ys_recv.at[z_to],
                    device_id={"row": y_peer},
                    device_id_type=MESH,
                )
            )

    def wait_y(z_to):
        pltpu.make_async_remote_copy(
            src_ref=part_y.at[z_to],
            dst_ref=got_y.at[z_to],
            send_sem=ys_send.at[z_to],
            recv_sem=ys_recv.at[z_to],
            device_id={"row": y_peer},
            device_id_type=MESH,
        ).wait_recv()

    def z_copy(source_z, target_z):
        return pltpu.make_async_remote_copy(
            src_ref=part_z.at[target_z],
            dst_ref=got_z.at[source_z],
            send_sem=zs_send.at[target_z],
            recv_sem=zs_recv.at[source_z],
            device_id={"row": target_z * 2 + my_y},
            device_id_type=MESH,
        )

    def to_z(place):
        for q in range(per_slot):
            z_to = k_slot(place) * per_slot + q
            mine = z_to == my_z
            wait_y(z_to)
            for k_base in k_bases:
                acc = partial_right(z_to * 2 + my_y, k_base)
                for j in range(tr):
                    here = pl.ds(j * tc + k_base, ktile)
                    total = acc[j] + got_y[z_to, here, :].astype(f32)
                    part_z[z_to, here, :] = total.astype(bf16)
                    accr_all[z_to, here, :] = total
            start_if(jnp.logical_not(mine), z_copy(my_z, z_to))

    def forward(delta):
        @pl.when(z_valid(delta))
        def _():
            right_copy(z_row(delta), fw_send.at[0], y_peer).wait_recv()

        sem = fw_send.at[2 * abs(delta) - 2 + (delta < 0)]
        start_if(z_valid(delta), right_copy(z_row(delta), sem, y_peer))

    def middle(step, carry):
        here = pl.ds(pl.multiple_of(step * 48, 48), 48)
        hidden_one, hidden_two = h1s[here, :], h2s[here, :]
        sig_one = sigmoid(hidden_one)
        h1s[here, :] = hidden_two * sig_one * (1.0 + hidden_one * (1.0 - sig_one))
        h2s[here, :] = hidden_one * sig_one
        return carry

    def gate_back(step, carry):
        here = pl.ds(pl.multiple_of(step * chunk, chunk), chunk)
        normed_out, _ = normalize(s_ref[here, :])
        gate_term = gts[here, :] * matmul(normed_out, woh, wol)
        gts[here, :] = matmul(gate_term, w5h, w5l, cols=(512, 640), transposed=True)
        return carry

    def left_back(step, carry):
        here = pl.ds(pl.multiple_of(step * chunk, chunk), chunk)
        scaled = accl[here, :] * lgm[here, :]
        wide = jnp.concatenate([scaled, scaled * lq[here, :]], axis=1)
        gts[here, :] += matmul(wide, w5h, w5l, cols=(0, 256), transposed=True)
        return carry

    def fold_left(owner, first):
        slot, offset = block_rows(owner)
        right32[...] = right_all[owner].astype(f32)
        for k_base in k_bases:

            def body(j, acc):
                tile = right32[pl.ds(pl.multiple_of(j * tc + k_base, 8), ktile), :]
                return tuple(
                    acc[i] + gp32[slot, pl.ds(i * tc + offset + j, 1), :] * tile for i in range(tr)
                )

            begin = tuple(
                jnp.zeros((ktile, 128), f32) if first else accl[pl.ds(i * tc + k_base, ktile), :] for i in range(tr)
            )
            acc = lax.fori_loop(0, tr, body, begin)
            for i in range(tr):
                accl[pl.ds(i * tc + k_base, ktile), :] = acc[i]

    to_y(places[0])
    arrive(places[1])
    to_y(places[1])
    lax.fori_loop(0, pairs // 48, middle, 0)
    lax.fori_loop(0, pairs // chunk, gate_back, 0)
    forward(1)
    forward(-1)
    to_z(places[0])
    for place in places[2:]:
        arrive(place)
        to_y(place)
    to_z(places[1])
    for far in range(2, n_z):
        forward(far)
        forward(-far)
        if far < len(places):
            to_z(places[far])
    for far in range(n_z, len(places)):
        to_z(places[far])

    def fold_if(delta):
        pl.when(z_valid(delta))(lambda: fold_left(z_row(delta), False))

    def fold_other(delta):
        @pl.when(z_valid(delta))
        def _():
            source = (my_z + delta) * 2 + (1 - my_y)
            right_copy(source, ag_send.at[0], y_peer).wait_recv()
            fold_left(source, False)

    deltas = [sign * far for far in range(1, n_z) for sign in (1, -1)]
    fold_left(row, True)
    fold_other(0)
    for delta in deltas:
        fold_if(delta)
    for delta in deltas:
        fold_other(delta)

    lax.fori_loop(0, pairs // chunk, left_back, 0)
    accr[...] = accr_all[my_z]
    for delta in deltas:

        @pl.when(z_valid(delta))
        def _():
            z_copy(my_z + delta, my_z + delta).wait_recv()
            accr[...] += got_z[my_z + delta].astype(f32)

    def back(step, carry):
        here = pl.ds(pl.multiple_of(step * chunk, chunk), chunk)
        right_scaled = accr[here, :] * rgm[here, :]
        wide = jnp.concatenate([right_scaled, right_scaled * rq[here, :]], axis=1)
        grad_mid = gts[here, :] + matmul(wide, w5h, w5l, cols=(256, 512), transposed=True)
        grad_updated = g_ref[here, :] + norm_back(nms[here, :], ims[here, :], grad_mid)
        grad_hidden = matmul(grad_updated, w3h, w3l, transposed=True, parts=2)
        both = jnp.concatenate([grad_hidden * h1s[here, :], grad_hidden * h2s[here, :]], axis=1)
        grad_normed_in = matmul(both, w12h, w12l, transposed=True, parts=2)
        normed_in, inv_in = normalize(x_ref[here, :])
        out_ref[here, :] = grad_updated + norm_back(normed_in, inv_in, grad_normed_in)
        return carry

    lax.fori_loop(0, pairs // chunk, back, 0)
    for copy in sends:
        copy.wait_send()
    for cond, copy in held:
        pl.when(cond)(copy.wait_send)


def per_device(mesh, pair_input, saved_product, pair_grad, token_mask, *weights):
    rows = mesh.shape["row"]
    n_col, n_ch = mesh.shape["col"], mesh.shape["ch"]
    tr, tc, width = pair_input.shape
    pairs = tr * tc
    tokens = token_mask.shape[0]
    hid = weights[0].shape[1]
    chunk = pairs // (pairs // (6 * 24)) if pairs % 144 == 0 else pairs
    ktile = 24 if tc % 24 == 0 else tc
    n_k, n_z = n_col * n_ch, rows // 2
    flat = [array.reshape(pairs, width) for array in (pair_input, saved_product, pair_grad)]
    arrays = [*flat, token_mask.reshape(1, tokens), *weights]
    vmem = pltpu.VMEM
    dma = pltpu.SemaphoreType.DMA
    tile32 = vmem((pairs, width), f32)
    sizes = (rows, pairs, tr, tc, tokens, n_col, n_ch, chunk, ktile)
    out = pl.pallas_call(
        functools.partial(kernel, sizes),
        out_shape=jax.ShapeDtypeStruct((pairs, width), f32),
        in_specs=[pl.BlockSpec(memory_space=pl.ANY)] * 13,
        out_specs=pl.BlockSpec(memory_space=vmem),
        scratch_shapes=[
            vmem((width, 2 * hid), bf16),
            vmem((width, 2 * hid), bf16),
            vmem((hid, width), bf16),
            vmem((hid, width), bf16),
            vmem((width, 5 * width), bf16),
            vmem((width, 5 * width), bf16),
            vmem((width, width), bf16),
            vmem((width, width), bf16),
            vmem((pairs, hid), f32),
            vmem((pairs, hid), f32),
            *([tile32] * 10),
            vmem((n_k, pairs, width), f32),
            tile32,
            tile32,
            vmem((n_z, pairs, width), f32),
            vmem((n_k, pairs, width), bf16),
            vmem((rows, pairs, width), bf16),
            *([vmem((n_z, pairs, width), bf16)] * 4),
            dma((2 * n_z,)),
            dma((rows,)),
            dma((2 * n_z,)),
            dma((n_k,)),
            dma((n_k,)),
            *([dma((n_z,))] * 4),
            dma((13,)),
            *[vmem(array.shape, array.dtype) for array in arrays],
        ],
        compiler_params=pltpu.CompilerParams(
            collective_id=0, has_side_effects=True, vmem_limit_bytes=56 * 1024 * 1024
        ),
    )(*arrays)
    return out.reshape(tr, tc, width)


def solution(mesh):
    tile = P(("grp", "row"), ("col", "ch"), None)
    in_specs = (tile, tile, tile, P("grp")) + (P(),) * 9
    return jax.shard_map(
        functools.partial(per_device, mesh), mesh=mesh, in_specs=in_specs, out_specs=tile, check_vma=False
    )
```

time: 30.9 us -> 28.8 us (0.932)
  Pallas kernels: 29.1 us -> 27.1 us
    pallas_call x1, Pallas kernels: 29.1 us -> 27.1 us  [per_device(): pl.pallas_call(functools.partial(kernel, sizes), out_shape=jax.ShapeDtype...]
where the time goes in v2:
time: 28.8 us; the launch traced here: 28.6 us
  Pallas kernels  27.1 us (94%)
  local copies, waits for them, and re-layouts  1.58 us (5%)
    pallas_call x1, Pallas kernels, per_device(): pl.pallas_call(functools.partial(kernel, sizes), out_shape=jax.ShapeDtype...  27.1 us
    unnamed x1, local copies, waits for them, and re-layouts  1.58 us

profile of v2, /device:TPU:0, one launch (start us, length us, event | category | flops | bytes accessed | tf_op | source)
XLA Modules:
  0.0 28.6 jit_solution(4334187212831435593)
XLA Ops:
  0.0 27.1 %shard_map.127 = f32[288,128]{1,0:T(8,128)} custom-call(f32[288,128]{1,0:T(8,128)} %bitcast.6, f32[288,128]{1,0:T(8,128)} %bitcast.7, f32[288,128]{1,0:T(8,128)} %bitcast.8, s32[1,96]{1,0:T(1,128)} %bitcast.9, f32[128,512]{1,0:T(8,128)} %w1_in.1, f32[128,512]{1,0:T(8,128)} %w2_in.1, f32[512,128]{1,0:T(8,128)} %w3_in.1, f32[128,128]{1,0:T(8,128)} %wl_in.1, ...), custom_call_target="tpu_custom_call" | custom-call | tf_op jit(solution)/shard_map/pallas_call | solution.py:515
  27.1 1.6 %copy.15 = f32[12,24,128]{2,1,0:T(8,128)} copy(f32[12,24,128]{2,1,0:T(8,128)} %bitcast.5) | data formatting | bytes 294912
